TPU v7x, 512 devices: a whole 4x8x8 slice. The times are simulated.
512 devices in a mesh: rows: 32 (over x, z), cols: 16 (over y, core).
Axes of the slice: x: 4, y: 8, z: 8, core: 2. Of those that a mesh axis runs over, the one named last changes fastest.
Arguments:
- points: float32 [3, 131072], P(None, 'rows'), as said below
- targets: float32 [16, 131072], P(None, 'rows'), may hold values from -6 to 6
- landmarks: int32 [256], replicated, may hold values from 0 to 131071
- neighbours: int32 [1024, 18], P('rows'), may hold values from 0 to 1023, as said below
- counts: int32 [1024], P('rows'), may hold values from 1 to 18
- core_inverse: float32 [256, 256], replicated, as said below
Outputs:
- solution: float32 [16, 131072], P(None, 'rows')
- residual: float32 [16, 131072], P(None, 'rows')
Inputs may be any that keep to these rules, and one draw needn't show every extreme that they name: `neighbours`: for block b the first counts[b] entries are distinct blocks in ascending order, b among them, each within 12 blocks of b; b lists c exactly when c lists b; the remaining slots hold b. `points`: points of blocks that do not list each other are farther apart than 1. `core_inverse`: Symmetric; each diagonal entry exceeds the sum of the magnitudes of the other entries of its row.
All inputs are finite; a program needn't handle non-finite values.
Results may differ from a plain program's by a relative error of at most 0.0003.
Values sent between devices are 32-bit elements; how exact they have to be, the bound alone decides.
A program may use at most 64 MiB of HBM per device.

v0:
```python
import jax
import jax.numpy as jnp
from jax import lax
from jax.sharding import PartitionSpec as P

MOST = 6
ITERS = 2
kernel_scale = 0.03125
ridge_shift = 1.0
tile_group = 32


def extended(cells, sides, width):
    for axis, dim in sides:
        count = lax.axis_size(axis)
        ends = count - 1
        head = lax.slice_in_dim(cells, 0, width, axis=dim)
        tail = lax.slice_in_dim(cells, cells.shape[dim] - width, cells.shape[dim], axis=dim)
        cells = jnp.concatenate(
            [
                lax.ppermute(tail, axis, [(i, (i + 1) % count) for i in range(ends)]),
                cells,
                lax.ppermute(head, axis, [((i + 1) % count, i) for i in range(ends)]),
            ],
            axis=dim,
        )
    return cells


def wendland(squared):
    distance = jnp.sqrt(squared)
    remain = jnp.maximum(1.0 - distance, 0.0)
    return remain * remain * remain * remain * (4.0 * distance + 1.0)


def squared_gap(first_pts, second_pts):
    offsets = first_pts[:, :, None] - second_pts[:, None, :]
    return jnp.sum(offsets * offsets, axis=0)


def tile_products(vector_halo, point_halo, row_points, nearby, amounts, last_tile):
    block_count = row_points.shape[1]
    block_width = row_points.shape[2]
    slot_count = nearby.shape[1]
    tile_ends = jnp.cumsum(amounts)
    tile_starts = tile_ends - amounts
    lane_ids = jnp.arange(tile_group, dtype=jnp.int32)
    block_ids = jnp.arange(block_count, dtype=jnp.int32)
    turn_count = (last_tile + tile_group - 1) // tile_group

    def advance(turn_index, running):
        position = turn_index * tile_group + lane_ids
        inside = position < last_tile
        owner_block = jnp.sum((tile_ends[None, :] <= position[:, None]).astype(jnp.int32), axis=1)
        owner_block = jnp.minimum(owner_block, block_count - 1)
        column = jnp.clip(position - tile_starts[owner_block], 0, slot_count - 1)
        partner = nearby[owner_block, column]
        row_side = row_points[:, owner_block]
        col_side = point_halo[:, partner]
        offsets = row_side[:, :, :, None] - col_side[:, :, None, :]
        kernel_tiles = wendland(jnp.sum(offsets * offsets, axis=0)) * inside[:, None, None].astype(
            jnp.float32
        )
        contrib = jnp.einsum(
            "ogn,gmn->ogm", vector_halo[:, partner], kernel_tiles, precision=lax.Precision.HIGHEST
        )
        placing = ((owner_block[:, None] == block_ids[None, :]) & inside[:, None]).astype(
            jnp.float32
        )
        return running + jnp.einsum(
            "ogm,gb->obm", contrib, placing, precision=lax.Precision.HIGHEST
        )

    start_total = jnp.zeros((vector_halo.shape[0], block_count, block_width), jnp.float32)
    return lax.fori_loop(0, turn_count, advance, start_total)


def body(points, targets, landmarks, neighbours, counts, core_inverse):
    col_count = lax.axis_size("cols")
    row_index = lax.axis_index("rows")
    col_index = lax.axis_index("cols")
    block_count = neighbours.shape[0]
    slab_points = points.shape[1]
    block_width = slab_points // block_count
    share_blocks = block_count // col_count
    share_points = share_blocks * block_width
    outputs_count = targets.shape[0]
    reach = 2 * MOST
    first_block = row_index * block_count
    local_ids = landmarks - row_index * slab_points
    present = (local_ids >= 0) & (local_ids < slab_points)
    picked = jnp.take(points, jnp.clip(local_ids, 0, slab_points - 1), axis=1) * present[
        None, :
    ].astype(jnp.float32)
    landmark_coords = lax.psum(picked, "rows")
    share_start = col_index * share_points
    own_points = lax.dynamic_slice_in_dim(points, share_start, share_points, 1)
    landmark_kernel = kernel_scale * wendland(squared_gap(landmark_coords, own_points))

    def precondition_share(residual_share):
        projected = jnp.dot(residual_share, landmark_kernel.T, precision=lax.Precision.HIGHEST)
        projected = lax.psum(projected, ("rows", "cols"))
        weights = jnp.dot(projected, core_inverse, precision=lax.Precision.HIGHEST)
        shared = residual_share - jnp.dot(weights, landmark_kernel, precision=lax.Precision.HIGHEST)
        product = lax.psum(jnp.sum(residual_share * shared, axis=1), ("rows", "cols"))
        return (shared, product)

    point_halo = extended(points, (("rows", 1),), reach * block_width)
    point_halo = point_halo.reshape(3, -1, block_width)
    nearby = neighbours - (first_block - reach)

    def share_of(vector):
        return lax.dynamic_slice_in_dim(vector, share_start, share_points, 1)

    def precondition(residual):
        shared, product = precondition_share(share_of(residual))
        return (lax.all_gather(shared, "cols", axis=1, tiled=True), product)

    solution = jnp.zeros_like(targets)
    residual = targets
    preconditioned, current = precondition(residual)
    direction = preconditioned
    for iteration in range(ITERS):
        vector_halo = extended(direction, (("rows", 1),), reach * block_width)
        vector_halo = vector_halo.reshape(outputs_count, -1, block_width)
        own_lists = lax.dynamic_slice_in_dim(nearby, col_index * share_blocks, share_blocks, 0)
        amounts = lax.dynamic_slice_in_dim(counts, col_index * share_blocks, share_blocks, 0)
        rows_here = own_points.reshape(3, share_blocks, block_width)
        tile_total = jnp.sum(amounts)
        partial_rows = tile_products(
            vector_halo, point_halo, rows_here, own_lists, amounts, tile_total
        )
        operate_product = lax.all_gather(
            partial_rows.reshape(outputs_count, share_points), "cols", axis=1, tiled=True
        )
        applied = kernel_scale * operate_product + ridge_shift * direction
        curvature_part = jnp.sum(share_of(direction) * share_of(applied), axis=1)
        step_size = current / lax.psum(curvature_part, ("rows", "cols"))
        solution = solution + step_size[:, None] * direction
        residual = residual - step_size[:, None] * applied
        if iteration + 1 < ITERS:
            preconditioned, following = precondition(residual)
            direction = preconditioned + (following / current)[:, None] * direction
            current = following
    solution, residual = (solution, residual)
    return (solution, residual)


def solution(mesh):
    placed = (P(None, "rows"), P(None, "rows"), P(), P("rows", None), P("rows"), P())
    return jax.shard_map(
        body,
        mesh=mesh,
        in_specs=placed,
        out_specs=(P(None, "rows"), P(None, "rows")),
        check_vma=False,
    )
```

profile of v0, /device:TPU:1, one launch (start us, length us, event | category | flops | bytes accessed | tf_op | source)
XLA Modules:
  0.0 767.7 jit_solution(12587315131149481955)
XLA Ops:
  1.5 4.8 collective-permute-start
  6.3 1.3 collective-permute-start.1
  7.6 1.5 copy.37
  10.1 121.2 %psum.49 = f32[3,256]{0,1:T(8,128)S(1)} all-reduce(f32[3,256]{0,1:T(8,128)S(1)} %multiply_bitcast_fusion), channel_id=1, replica_groups=mesh['rows'=32,'cols'=16] {'rows'}, use_global_device_ids=true, to_apply=%region_0.1 | all-reduce | flops 768 | bytes 6144 | tf_op jit(solution)/shard_map/psum | solution.py:95
  132.0 124.0 %psum.50 = f32[16,256]{1,0:T(8,128)S(1)} all-reduce(f32[16,256]{1,0:T(8,128)S(1)} %fusion.84), channel_id=1, replica_groups=mesh['rows'=32,'cols'=16] {'rows','cols'}, use_global_device_ids=true, to_apply=%region_2.3 | all-reduce | flops 4096 | bytes 32768 | tf_op jit(solution)/shard_map/psum | solution.py:102
  256.7 16.2 %all_gather.12 = f32[16,4096]{1,0:T(8,128)S(1)} all-gather(f32[16,256]{1,0:T(8,128)S(1)} %get-tuple-element.306), channel_id=1, replica_groups=mesh['rows'=32,'cols'=16] {'cols'}, dimensions={1}, use_global_device_ids=true | all-gather | bytes 278528 | tf_op jit(solution)/shard_map/all_gather | solution.py:117
  272.9 2.8 collective-permute-start.2
  275.7 1.3 collective-permute-start.3
  279.0 2.5 collective-permute-done.3
  281.6 12.1 %while.22 = (s32[]{:T(128)}, f32[16,2,128]{2,1,0:T(2,128)S(1)}, s32[]{:T(128)}, s32[2]{0:T(128)S(1)}, s32[]{:T(128)}, /*index=5*/f32[3,2,128]{2,0,1:T(4,128)S(1)...) while((s32[]{:T(128)}, f32[16,2,128]{2,1,0:T(2,128)S(1)}, ...), condition=%wide.region_10.11_spmd.clone, body=%wide.region_7.10_spmd.clone.sunk | while | flops 111156288 | bytes 6040561 | solution.py:75
  287.0 2.1 multiply_reduce_fusion.9
  289.0 4.3 fusion.139
  293.7 16.3 %all_gather.13 = f32[16,4096]{1,0:T(8,128)S(1)} all-gather(f32[16,256]{1,0:T(8,128)S(1)} %bitcast.164), channel_id=1, replica_groups=mesh['rows'=32,'cols'=16] {'cols'}, dimensions={1}, use_global_device_ids=true | all-gather | bytes 278528 | tf_op jit(solution)/shard_map/all_gather | solution.py:133
  310.1 104.1 %all-reduce = (f32[16]{0:T(128)S(1)}, f32[16]{0:T(128)S(1)}) all-reduce(f32[16]{0:T(128)S(1)} %get-tuple-element.305, f32[16]{0:T(128)S(1)} %multiply_reduce_fusion.5), channel_id=1, replica_groups=mesh['rows'=32,'cols'=16] {'rows','cols'}, use_global_device_ids=true, to_apply=%region_4.5 | all-reduce | flops 32 | bytes 256 | tf_op jit(solution)/shard_map/psum | solution.py:105
  414.7 94.7 %psum.53 = f32[16,256]{1,0:T(8,128)S(1)} all-reduce(f32[16,256]{1,0:T(8,128)S(1)} %fusion.82), channel_id=1, replica_groups=mesh['rows'=32,'cols'=16] {'rows','cols'}, use_global_device_ids=true, to_apply=%region_13.14 | all-reduce | flops 4096 | bytes 32768 | tf_op jit(solution)/shard_map/psum | solution.py:102
  510.1 95.3 %psum.54 = f32[16]{0:T(128)S(1)} all-reduce(f32[16]{0:T(128)S(1)} %get-tuple-element.307), channel_id=1, replica_groups=mesh['rows'=32,'cols'=16] {'rows','cols'}, use_global_device_ids=true, to_apply=%region_15.16 | all-reduce | flops 16 | bytes 128 | tf_op jit(solution)/shard_map/psum | solution.py:105
  605.4 18.2 %all_gather.14 = f32[16,4096]{1,0:T(8,128)S(1)} all-gather(f32[16,256]{1,0:T(8,128)S(1)} %get-tuple-element.308), channel_id=1, replica_groups=mesh['rows'=32,'cols'=16] {'cols'}, dimensions={1}, use_global_device_ids=true | all-gather | bytes 278528 | tf_op jit(solution)/shard_map/all_gather | solution.py:117
  623.7 1.7 collective-permute-start.4
  627.4 4.6 collective-permute-done.5
  632.1 12.0 %while.23 = (s32[]{:T(128)}, f32[16,2,128]{2,1,0:T(2,128)S(1)}, s32[]{:T(128)}, s32[2]{0:T(128)S(1)}, s32[]{:T(128)}, /*index=5*/f32[3,2,128]{2,0,1:T(4,128)S(1)...) while((s32[]{:T(128)}, f32[16,2,128]{2,1,0:T(2,128)S(1)}, ...), condition=%wide.region_19.20_spmd.clone, body=%wide.region_16.19_spmd.clone.sunk | while | flops 111156288 | bytes 6040561 | solution.py:75
  637.4 2.1 multiply_reduce_fusion.10
  639.5 4.3 fusion.150
  644.1 17.1 %all_gather.15 = f32[16,4096]{1,0:T(8,128)S(1)} all-gather(f32[16,256]{1,0:T(8,128)S(1)} %bitcast.165), channel_id=1, replica_groups=mesh['rows'=32,'cols'=16] {'cols'}, dimensions={1}, use_global_device_ids=true | all-gather | bytes 278528 | tf_op jit(solution)/shard_map/all_gather | solution.py:133
  661.4 105.4 %psum.55 = f32[16]{0:T(128)S(1)} all-reduce(f32[16]{0:T(128)S(1)} %multiply_reduce_fusion.3), channel_id=1, replica_groups=mesh['rows'=32,'cols'=16] {'rows','cols'}, use_global_device_ids=true, to_apply=%region_21.22 | all-reduce | flops 16 | bytes 128 | tf_op jit(solution)/shard_map/psum | solution.py:138
  (88 shorter events, 20.0 us)
Async XLA Ops:
  0.6 255.4 %copy-start = (f32[256,256]{1,0:T(8,128)S(1)}, f32[256,256]{1,0:T(8,128)}, u32[]{:S(2)}) copy-start(f32[256,256]{1,0:T(8,128)} %param.15) | copy-start | bytes 786436
  0.6 8.5 %copy-start.1 = (f32[3,4096]{1,0:T(4,128)S(1)}, f32[3,4096]{1,0:T(4,128)}, u32[]{:S(2)}) copy-start(f32[3,4096]{1,0:T(4,128)} %param.10) | copy-start | bytes 147460
  0.7 8.5 %copy-start.4 = (s32[256]{0:T(256)S(1)}, s32[256]{0:T(256)}, u32[]{:S(2)}) copy-start(s32[256]{0:T(256)} %param.12) | copy-start | bytes 3076
  0.7 130.9 %copy-start.2 = (f32[16,4096]{1,0:T(8,128)S(1)}, f32[16,4096]{1,0:T(8,128)}, u32[]{:S(2)}) copy-start(f32[16,4096]{1,0:T(8,128)} %param.11) | copy-start | bytes 786436
  1.5 277.5 %collective-permute-start = (f32[3,1536]{1,0:T(4,128)S(1)}, f32[3,1536]{1,0:T(4,128)S(1)}, u32[]{:S(2)}, u32[]{:S(2)}) collective-permute-start(f32[3,1536]{1,0:T(4,128)S(1)} %get-tuple-element.298), channel_id=1, source_target_pairs={{0,16},{16,32},{32,48},{48,64},{64,80},{80,96},{96,112},{112,128},... | collective-permute-start | bytes 55304 | tf_op jit(solution)/shard_map/ppermute | solution.py:21
  6.3 272.6 %collective-permute-start.1 = (f32[3,1536]{1,0:T(4,128)S(1)}, f32[3,1536]{1,0:T(4,128)S(1)}, u32[]{:S(2)}, u32[]{:S(2)}) collective-permute-start(f32[3,1536]{1,0:T(4,128)S(1)} %get-tuple-element.299), channel_id=1, source_target_pairs={{16,0},{32,16},{48,32},{64,48},{80,64},{96,80},{112,96},{128,112},... | collective-permute-start | bytes 55304 | tf_op jit(solution)/shard_map/ppermute | solution.py:23
  9.1 267.9 %copy-start.5 = (s32[32]{0:T(128)S(1)}, s32[32]{0:T(128)}, u32[]{:S(2)}) copy-start(s32[32]{0:T(128)} %param.14) | copy-start | bytes 388
  9.1 269.0 %copy-start.3 = (s32[32,18]{0,1:T(8,128)S(1)}, s32[32,18]{0,1:T(8,128)}, u32[]{:S(2)}) copy-start(s32[32,18]{0,1:T(8,128)} %param.13) | copy-start | bytes 6916
  272.9 6.1 collective-permute-start.2
  275.7 5.8 collective-permute-start.3
  623.7 3.6 collective-permute-start.4
  625.4 6.6 collective-permute-start.5
where the time goes:
time: 769 us; the launch traced here: 768 us
  blocking collectives  713 us (93%)
  starting transfers between devices  13.1 us (2%)
  matrix products  11.3 us (1%)
  other arithmetic  11.2 us (1%)
  local copies, waits for them, and re-layouts  9.75 us (1%)
  waiting for transfers between devices  7.82 us (1%)
    psum x2, blocking collectives, precondition_share(): projected = lax.psum(projected, ('rows', 'cols'))  219 us
    psum x2, blocking collectives, precondition_share(): lax.psum(jnp.sum(residual_share * shared, axis=1), ('rows', 'cols'))  199 us
    psum x1, blocking collectives, body(): landmark_coords = lax.psum(picked, 'rows')  121 us
    psum x1, blocking collectives, body(): step_size = current / lax.psum(curvature_part, ('rows', 'cols'))  105 us
    all_gather x2, blocking collectives, precondition(): return (lax.all_gather(shared, 'cols', axis=1, tiled=True), product)  34.4 us
    all_gather x2, blocking collectives, body(): lax.all_gather(partial_rows.reshape(outputs_count, share_points), 'cols',...  33.5 us
  transfers between devices with their start and end apart: 6, of which 3 were waited for; matrix products, arithmetic and copies ran while one was open for 1% of the time, Pallas kernels for 0%

commit v1 on v0

--- a/solution.py
+++ b/solution.py
@@ -92,7 +92,11 @@
     picked = jnp.take(points, jnp.clip(local_ids, 0, slab_points - 1), axis=1) * present[
         None, :
     ].astype(jnp.float32)
-    landmark_coords = lax.psum(picked, "rows")
+    landmark_coords = picked
+    for hop in (1, 2, 4, 8, 16):
+        landmark_coords = landmark_coords + lax.ppermute(
+            landmark_coords, "rows", [(dev, dev ^ hop) for dev in range(32)]
+        )
     share_start = col_index * share_points
     own_points = lax.dynamic_slice_in_dim(points, share_start, share_points, 1)
     landmark_kernel = kernel_scale * wendland(squared_gap(landmark_coords, own_points))

time: 769 us -> 673 us (0.88)
  blocking collectives: 713 us -> 571 us
  starting transfers between devices: 13.1 us -> 37 us
  waiting for transfers between devices: 7.82 us -> 30.1 us
    psum x1 -> x0, blocking collectives: 121 us -> none  [body(): landmark_coords = lax.psum(picked, 'rows')]
    ppermute x0 -> x5, starting transfers between devices: none -> 23.9 us  [body(): lax.ppermute(landmark_coords, 'rows', [(dev, dev ^ hop) for dev in range(...]
    psum x2, blocking collectives: 219 us -> 197 us  [precondition_share(): projected = lax.psum(projected, ('rows', 'cols'))]
    ppermute x0 -> x5, waiting for transfers between devices: none -> 20.4 us  [body(): lax.ppermute(landmark_coords, 'rows', [(dev, dev ^ hop) for dev in range(...]
  transfers between devices with their start and end apart: 6 -> 11, of which waited for: 3 -> 9; matrix products, arithmetic and copies ran while one was open for 1% -> 1% of each run, Pallas kernels for 0% -> 0%
where the time goes in v1:
time: 673 us; the launch traced here: 672 us
  blocking collectives  571 us (85%)
  starting transfers between devices  37 us (5%)
  waiting for transfers between devices  30.1 us (4%)
  other arithmetic  11.4 us (2%)
  matrix products  11.3 us (2%)
  local copies, waits for them, and re-layouts  9.78 us (1%)
    psum x2, blocking collectives, precondition_share(): lax.psum(jnp.sum(residual_share * shared, axis=1), ('rows', 'cols'))  200 us
    psum x2, blocking collectives, precondition_share(): projected = lax.psum(projected, ('rows', 'cols'))  197 us
    psum x1, blocking collectives, body(): step_size = current / lax.psum(curvature_part, ('rows', 'cols'))  105 us
    all_gather x2, blocking collectives, precondition(): return (lax.all_gather(shared, 'cols', axis=1, tiled=True), product)  34.3 us
    all_gather x2, blocking collectives, body(): lax.all_gather(partial_rows.reshape(outputs_count, share_points), 'cols',...  33.5 us
    ppermute x5, starting transfers between devices, body(): lax.ppermute(landmark_coords, 'rows', [(dev, dev ^ hop) for dev in range(...  23.9 us
    ppermute x5, waiting for transfers between devices, body(): lax.ppermute(landmark_coords, 'rows', [(dev, dev ^ hop) for dev in range(...  20.4 us
  transfers between devices with their start and end apart: 11, of which 9 were waited for; matrix products, arithmetic and copies ran while one was open for 1% of the time, Pallas kernels for 0%

profile of v1, /device:TPU:1, one launch (start us, length us, event | category | flops | bytes accessed | tf_op | source)
XLA Modules:
  0.0 672.2 jit_solution(13217513233991936336)
XLA Ops:
  1.5 4.8 collective-permute-start.5
  10.1 4.6 collective-permute-start
  17.2 7.6 %collective-permute-start.1 = (f32[3,256]{0,1:T(8,128)S(1)}, f32[3,256]{0,1:T(8,128)S(1)}, u32[]{:S(2)}, u32[]{:S(2)}) collective-permute-start(f32[3,256]{0,1:T(8,128)S(1)} %fusion.108), channel_id=1, source_target_pairs={{0,32},{16,48},{32,0},{48,16},{64,96},{80,112},{96,64},{112,80},{1... | collective-permute-start | bytes 9224 | tf_op jit(solution)/shard_map/ppermute | solution.py:97
  25.6 5.4 collective-permute-done.1
  30.9 4.6 collective-permute-start.2
  35.6 7.8 %collective-permute-done.2 = f32[3,256]{0,1:T(8,128)S(1)} collective-permute-done((f32[3,256]{0,1:T(8,128)S(1)}, f32[3,256]{0,1:T(8,128)S(1)}, u32[]{:S(2)}, u32[]{:S(2)}) %collective-permute-start.2) | collective-permute-done | bytes 3104 | tf_op jit(solution)/shard_map/ppermute | solution.py:97
  43.4 2.8 collective-permute-start.3
  46.2 2.9 collective-permute-done.3
  49.1 4.3 collective-permute-start.4
  57.3 102.4 %psum.42 = f32[16,256]{1,0:T(8,128)S(1)} all-reduce(f32[16,256]{1,0:T(8,128)S(1)} %fusion.84), channel_id=1, replica_groups=mesh['rows'=32,'cols'=16] {'rows','cols'}, use_global_device_ids=true, to_apply=%region_1.2 | all-reduce | flops 4096 | bytes 32768 | tf_op jit(solution)/shard_map/psum | solution.py:106
  160.4 16.3 %all_gather.12 = f32[16,4096]{1,0:T(8,128)S(1)} all-gather(f32[16,256]{1,0:T(8,128)S(1)} %get-tuple-element.306), channel_id=1, replica_groups=mesh['rows'=32,'cols'=16] {'cols'}, dimensions={1}, use_global_device_ids=true | all-gather | bytes 278528 | tf_op jit(solution)/shard_map/all_gather | solution.py:121
  181.4 3.8 collective-permute-done.8
  185.2 12.1 %while.22 = (s32[]{:T(128)}, f32[16,2,128]{2,1,0:T(2,128)S(1)}, s32[]{:T(128)}, s32[2]{0:T(128)S(1)}, s32[]{:T(128)}, /*index=5*/f32[3,2,128]{2,0,1:T(4,128)S(1)...) while((s32[]{:T(128)}, f32[16,2,128]{2,1,0:T(2,128)S(1)}, ...), condition=%wide.region_9.10_spmd.clone, body=%wide.region_6.9_spmd.clone.sunk | while | flops 111156288 | bytes 6040561 | solution.py:75
  192.7 4.3 fusion.140
  197.3 16.4 %all_gather.13 = f32[16,4096]{1,0:T(8,128)S(1)} all-gather(f32[16,256]{1,0:T(8,128)S(1)} %bitcast.166), channel_id=1, replica_groups=mesh['rows'=32,'cols'=16] {'cols'}, dimensions={1}, use_global_device_ids=true | all-gather | bytes 278528 | tf_op jit(solution)/shard_map/all_gather | solution.py:137
  213.8 104.8 %all-reduce = (f32[16]{0:T(128)S(1)}, f32[16]{0:T(128)S(1)}) all-reduce(f32[16]{0:T(128)S(1)} %get-tuple-element.305, f32[16]{0:T(128)S(1)} %multiply_reduce_fusion.5), channel_id=1, replica_groups=mesh['rows'=32,'cols'=16] {'rows','cols'}, use_global_device_ids=true, to_apply=%region_3.4 | all-reduce | flops 32 | bytes 256 | tf_op jit(solution)/shard_map/psum | solution.py:109
  319.2 94.7 %psum.45 = f32[16,256]{1,0:T(8,128)S(1)} all-reduce(f32[16,256]{1,0:T(8,128)S(1)} %fusion.82), channel_id=1, replica_groups=mesh['rows'=32,'cols'=16] {'rows','cols'}, use_global_device_ids=true, to_apply=%region_12.13 | all-reduce | flops 4096 | bytes 32768 | tf_op jit(solution)/shard_map/psum | solution.py:106
  414.5 95.5 %psum.46 = f32[16]{0:T(128)S(1)} all-reduce(f32[16]{0:T(128)S(1)} %get-tuple-element.307), channel_id=1, replica_groups=mesh['rows'=32,'cols'=16] {'rows','cols'}, use_global_device_ids=true, to_apply=%region_14.15 | all-reduce | flops 16 | bytes 128 | tf_op jit(solution)/shard_map/psum | solution.py:109
  510.0 18.0 %all_gather.14 = f32[16,4096]{1,0:T(8,128)S(1)} all-gather(f32[16,256]{1,0:T(8,128)S(1)} %get-tuple-element.308), channel_id=1, replica_groups=mesh['rows'=32,'cols'=16] {'cols'}, dimensions={1}, use_global_device_ids=true | all-gather | bytes 278528 | tf_op jit(solution)/shard_map/all_gather | solution.py:121
  531.8 4.6 collective-permute-done.10
  536.5 12.0 %while.23 = (s32[]{:T(128)}, f32[16,2,128]{2,1,0:T(2,128)S(1)}, s32[]{:T(128)}, s32[2]{0:T(128)S(1)}, s32[]{:T(128)}, /*index=5*/f32[3,2,128]{2,0,1:T(4,128)S(1)...) while((s32[]{:T(128)}, f32[16,2,128]{2,1,0:T(2,128)S(1)}, ...), condition=%wide.region_18.19_spmd.clone, body=%wide.region_15.18_spmd.clone.sunk | while | flops 111156288 | bytes 6040561 | solution.py:75
  544.0 4.3 fusion.151
  548.6 17.1 %all_gather.15 = f32[16,4096]{1,0:T(8,128)S(1)} all-gather(f32[16,256]{1,0:T(8,128)S(1)} %bitcast.167), channel_id=1, replica_groups=mesh['rows'=32,'cols'=16] {'cols'}, dimensions={1}, use_global_device_ids=true | all-gather | bytes 278528 | tf_op jit(solution)/shard_map/all_gather | solution.py:137
  565.9 105.4 %psum.47 = f32[16]{0:T(128)S(1)} all-reduce(f32[16]{0:T(128)S(1)} %multiply_reduce_fusion.3), channel_id=1, replica_groups=mesh['rows'=32,'cols'=16] {'rows','cols'}, use_global_device_ids=true, to_apply=%region_20.21 | all-reduce | flops 16 | bytes 128 | tf_op jit(solution)/shard_map/psum | solution.py:142
  (102 shorter events, 37.8 us)
Async XLA Ops:
  0.6 159.0 %copy-start = (f32[256,256]{1,0:T(8,128)S(1)}, f32[256,256]{1,0:T(8,128)}, u32[]{:S(2)}) copy-start(f32[256,256]{1,0:T(8,128)} %param.15) | copy-start | bytes 786436
  0.6 45.6 %copy-start.1 = (f32[3,4096]{1,0:T(4,128)S(1)}, f32[3,4096]{1,0:T(4,128)}, u32[]{:S(2)}) copy-start(f32[3,4096]{1,0:T(4,128)} %param.10) | copy-start | bytes 147460
  0.7 8.5 %copy-start.4 = (s32[256]{0:T(256)S(1)}, s32[256]{0:T(256)}, u32[]{:S(2)}) copy-start(s32[256]{0:T(256)} %param.12) | copy-start | bytes 3076
  0.7 14.0 %copy-start.5 = (s32[32]{0:T(128)S(1)}, s32[32]{0:T(128)}, u32[]{:S(2)}) copy-start(s32[32]{0:T(128)} %param.14) | copy-start | bytes 388
  0.7 34.9 %copy-start.3 = (s32[32,18]{0,1:T(8,128)S(1)}, s32[32,18]{0,1:T(8,128)}, u32[]{:S(2)}) copy-start(s32[32,18]{0,1:T(8,128)} %param.13) | copy-start | bytes 6916
  1.5 179.2 %collective-permute-start.5 = (f32[3,1536]{1,0:T(4,128)S(1)}, f32[3,1536]{1,0:T(4,128)S(1)}, u32[]{:S(2)}, u32[]{:S(2)}) collective-permute-start(f32[3,1536]{1,0:T(4,128)S(1)} %get-tuple-element.298), channel_id=1, source_target_pairs={{0,16},{16,32},{32,48},{48,64},{64,80},{80,96},{96,112},{112,128},... | collective-permute-start | bytes 55304 | tf_op jit(solution)/shard_map/ppermute | solution.py:21
  6.3 174.4 %collective-permute-start.6 = (f32[3,1536]{1,0:T(4,128)S(1)}, f32[3,1536]{1,0:T(4,128)S(1)}, u32[]{:S(2)}, u32[]{:S(2)}) collective-permute-start(f32[3,1536]{1,0:T(4,128)S(1)} %get-tuple-element.299), channel_id=1, source_target_pairs={{16,0},{32,16},{48,32},{64,48},{80,64},{96,80},{112,96},{128,112},... | collective-permute-start | bytes 55304 | tf_op jit(solution)/shard_map/ppermute | solution.py:23
  7.6 49.3 %copy-start.2 = (f32[16,4096]{1,0:T(8,128)S(1)}, f32[16,4096]{1,0:T(8,128)}, u32[]{:S(2)}) copy-start(f32[16,4096]{1,0:T(8,128)} %param.11) | copy-start | bytes 786436
  10.1 7.0 %collective-permute-start = (f32[3,256]{0,1:T(8,128)S(1)}, f32[3,256]{0,1:T(8,128)S(1)}, u32[]{:S(2)}, u32[]{:S(2)}) collective-permute-start(f32[3,256]{0,1:T(8,128)S(1)} %multiply_bitcast_fusion), channel_id=1, source_target_pairs={{0,16},{16,0},{32,48},{48,32},{64,80},{80,64},{96,112},{112,96},{1... | collective-permute-start | bytes 9224 | tf_op jit(solution)/shard_map/ppermute | solution.py:97
  17.2 13.7 %collective-permute-start.1 = (f32[3,256]{0,1:T(8,128)S(1)}, f32[3,256]{0,1:T(8,128)S(1)}, u32[]{:S(2)}, u32[]{:S(2)}) collective-permute-start(f32[3,256]{0,1:T(8,128)S(1)} %fusion.108), channel_id=1, source_target_pairs={{0,32},{16,48},{32,0},{48,16},{64,96},{80,112},{96,64},{112,80},{1... | collective-permute-start | bytes 9224 | tf_op jit(solution)/shard_map/ppermute | solution.py:97
  30.9 12.5 %collective-permute-start.2 = (f32[3,256]{0,1:T(8,128)S(1)}, f32[3,256]{0,1:T(8,128)S(1)}, u32[]{:S(2)}, u32[]{:S(2)}) collective-permute-start(f32[3,256]{0,1:T(8,128)S(1)} %add.208), channel_id=1, source_target_pairs={{0,64},{16,80},{32,96},{48,112},{64,0},{80,16},{96,32},{112,48},{1... | collective-permute-start | bytes 9224 | tf_op jit(solution)/shard_map/ppermute | solution.py:97
  43.4 5.7 collective-permute-start.3
  49.1 7.5 %collective-permute-start.4 = (f32[3,256]{0,1:T(8,128)S(1)}, f32[3,256]{0,1:T(8,128)S(1)}, u32[]{:S(2)}, u32[]{:S(2)}) collective-permute-start(f32[3,256]{0,1:T(8,128)S(1)} %add.210), channel_id=1, source_target_pairs={{0,256},{16,272},{32,288},{48,304},{64,320},{80,336},{96,352},{112... | collective-permute-start | bytes 9224 | tf_op jit(solution)/shard_map/ppermute | solution.py:97
  176.7 4.7 collective-permute-start.7
  179.4 5.8 collective-permute-start.8
  528.2 3.6 collective-permute-start.9
  529.9 6.6 collective-permute-start.10
